TPU v7x, 256 devices: a whole 4x4x8 slice. The times are simulated.
256 devices in a mesh: batch: 128 (over z, y_lo, x, core), crop: 2 (over y_hi).
Axes of the slice: x: 4, y: 4 (y_hi: 2, y_lo: 2; y = y_hi * 2 + y_lo), z: 8, core: 2. Of those that a mesh axis runs over, the one named last changes fastest.
Arguments:
- voxels: bfloat16 [2, 131072, 512], P('crop', 'batch'), may hold values from -6 to 6
- phrases: bfloat16 [2048, 512], P('batch'), may hold values from -6 to 6
- pair_ids: int32 [2048], P('batch'), may hold values from 0 to 511
- margin_index: int32 [2, 128, 512], P('crop', 'batch'), may hold values from 0 to 1023, as said below
Outputs:
- voxel_grad: float32 [2, 131072, 512], P('crop', 'batch')
- phrase_grad: float32 [2048, 512], P('batch')
Inputs may be any that keep to these rules, and one draw needn't show every extreme that they name: Each list margin_index[c, b] holds 512 distinct rows of that batch index's 1024 rows; entry k of crop 0 and entry k of crop 1 at the same b show the same place.
All inputs are finite; a program needn't handle non-finite values.
Results may differ from a plain program's by a relative error of at most 0.0013.
Values may be sent and summed in bfloat16 or wider, within the bound.
A program may use at most 64 MiB of HBM per device.

v0:
```python
import math
import jax
import jax.numpy as jnp
from jax import lax
from jax.sharding import PartitionSpec as P

VOX_VOL = 256


def partner_2(value, axis, distance):
    mask = 2**distance
    pairs = [(source, source ^ mask) for source in range(lax.axis_size(axis))]
    return lax.ppermute(value, axis, pairs)


def local(voxels, phrases, pair_ids, margin_index):
    own_vox = voxels[0]
    rows, width = own_vox.shape
    scale = 1.0 / math.sqrt(width)
    owner_ids = lax.all_gather(pair_ids, "batch", axis=0, tiled=True)
    position = lax.axis_index("batch")
    volume = (position * rows + jnp.arange(rows, dtype=jnp.int32)) // VOX_VOL

    def tile(block, block_ids):
        sign = jnp.where(volume[:, None] == block_ids[None, :], 1.0, -1.0).astype(jnp.float32)
        logit = jnp.dot(own_vox, block.T, preferred_element_type=jnp.float32) * scale - 1.0
        dlogit = (-sign * jax.nn.sigmoid(-sign * logit)).astype(jnp.bfloat16)
        match_part = jnp.dot(dlogit, block, preferred_element_type=jnp.float32) * scale
        phrase_part = (
            lax.dot_general(
                dlogit, own_vox, (((0,), (0,)), ((), ())), preferred_element_type=jnp.float32
            )
            * scale
        )
        return (match_part, phrase_part)

    gathered = lax.all_gather(phrases, "batch", axis=0, tiled=True)
    total = gathered.shape[0]
    block_rows = math.gcd(total, 1024)
    num_blocks = total // block_rows
    blocks = gathered.reshape(num_blocks, block_rows, width)
    id_blocks = owner_ids.reshape(num_blocks, block_rows)

    def one_block(match_total, pieces):
        match_part, phrase_part = tile(pieces[0], pieces[1])
        return (match_total + match_part, phrase_part)

    match_grad, phrase_terms = lax.scan(
        one_block, jnp.zeros((rows, width), jnp.float32), (blocks, id_blocks)
    )
    own_partial = lax.psum_scatter(
        phrase_terms.reshape(total, width), "batch", scatter_dimension=0, tiled=True
    )
    phrase_grad = lax.psum(own_partial, "crop")
    picked = margin_index[0, 0]
    chosen = own_vox[picked]
    partner = partner_2(chosen, "crop", 0)
    voxel_grad = match_grad.at[picked].add(chosen.astype(jnp.float32) - partner.astype(jnp.float32))
    return (voxel_grad[None], phrase_grad)


def solution(mesh):
    placed = (P("crop", "batch", None), P("batch", None), P("batch"), P("crop", "batch", None))
    return jax.shard_map(
        local,
        mesh=mesh,
        in_specs=placed,
        out_specs=(P("crop", "batch", None), P("batch", None)),
        check_vma=False,
    )
```

profile of v0, /device:TPU:0, one launch (start us, length us, event | category | flops | bytes accessed | tf_op | source)
XLA Modules:
  0.0 844.9 jit_solution(14683347854786272296)
XLA Ops:
  7.2 0.0 all-gather.2.cloned.1.call-start
  7.2 0.7 all-gather.2.cloned.1.call-update
  7.9 0.0 reduce-scatter.2.cloned.1.call-start
  8.0 1.3 dynamic-slice
  10.0 0.9 dynamic-update-slice
  10.8 25.8 %all-reduce = s32[2048]{0:T(1024)S(1)} all-reduce(s32[2048]{0:T(1024)S(1)} %dynamic-update-slice), channel_id=1, replica_groups=mesh['batch'=128,'crop'=2] {'batch'}, use_global_device_ids=true, to_apply=%add | all-reduce | flops 2048 | bytes 16384
  36.6 188.7 %all-gather.2.cloned.1.call-done = bf16[2048,512]{1,0:T(8,128)(2,1)} async-done(((bf16[16,512]{1,0:T(8,128)(2,1)}), bf16[2048,512]{1,0:T(8,128)(2,1)}) %all-gather.2.cloned.1.call-update) | async-done | bytes 2097168 | tf_op jit(solution)/shard_map/all_gather | solution.py:37
  225.3 24.8 %while.15 = (s32[]{:T(128)}, f32[1024,512]{1,0:T(8,128)}, f32[2,1024,512]{2,1,0:T(8,128)}, s32[2,1024]{1,0:T(2,128)S(1)}, bf16[2,1024,512]{2,1,0:T(8,128)(2,1)},...) while((s32[]{:T(128)}, f32[1024,512]{1,0:T(8,128)}, ...), condition=%wide.region_1.2_spmd.clone, body=%wide.region_0.1_spmd.clone.sunk | while | flops 3234873344 | bytes 37770436 | solution.py:48
  225.3 0.0 copy-start
  225.4 3.9 fusion.38
  229.3 0.0 copy-start.4
  229.3 1.3 copy-done.4
  230.6 0.0 copy-done
  230.6 2.6 bitcast_dynamic-update-slice_fusion.2
  233.2 0.0 copy-done.3
  233.2 4.2 select_add_fusion.2
  237.5 0.0 copy-start
  237.5 3.9 fusion.38
  241.4 0.0 copy-start.4
  241.4 1.3 copy-done.4
  242.7 0.0 copy-done
  242.7 2.6 bitcast_dynamic-update-slice_fusion.2
  245.3 4.8 select_add_fusion.2
  250.1 0.0 reduce-scatter.2.cloned.1.call-update
  250.1 0.7 copy-done.2
  250.8 0.5 copy-done.1
  251.3 2.0 gather_fusion
  253.3 3.1 collective-permute-start
  256.4 11.9 %collective-permute-done = bf16[512,512]{1,0:T(8,128)(2,1)S(1)} collective-permute-done((bf16[512,512]{1,0:T(8,128)(2,1)S(1)}, bf16[512,512]{1,0:T(8,128)(2,1)S(1)}, u32[]{:S(2)}, u32[]{:S(2)}) %collective-permute-start) | collective-permute-done | bytes 524320 | tf_op jit(solution)/shard_map/ppermute | solution.py:13
  268.3 6.5 scatter_custom_fusion
  274.8 551.3 %reduce-scatter.2.cloned.1.call-done = f32[16,512]{1,0:T(8,128)} async-done(((f32[2048,512]{1,0:T(8,128)}), f32[16,512]{1,0:T(8,128)}) %reduce-scatter.2.cloned.1.call-update) | async-done | bytes 32784 | tf_op jit(solution)/shard_map/reduce_scatter | solution.py:51
  826.1 12.0 %psum.7 = f32[16,512]{1,0:T(8,128)} all-reduce(f32[16,512]{1,0:T(8,128)} %reduce-scatter.2.cloned.1.call-done), channel_id=1, replica_groups=mesh['batch'=128,'crop'=2] {'crop'}, use_global_device_ids=true, to_apply=%region_4.5 | all-reduce | flops 8192 | bytes 65536 | tf_op jit(solution)/shard_map/psum | solution.py:54
  (15 shorter events, 0.1 us)
Async XLA Ops:
  7.2 218.2 %all-gather.2.cloned.1.call-start = ((), (), s32[]{:S(2)}) async-start(), calls=%async_computation.1 | async-start | bytes 2113536 | tf_op jit(solution)/shard_map/all_gather | solution.py:37
  7.9 818.2 %reduce-scatter.2.cloned.1.call-start = ((), (), s32[]{:S(2)}) async-start(), calls=%async_computation.2 | async-start | bytes 4227072 | tf_op jit(solution)/shard_map/reduce_scatter | solution.py:51
  225.3 5.3 copy-start
  229.3 1.3 copy-start.4
  230.6 2.6 copy-start.3
  237.5 5.3 copy-start
  241.4 1.3 copy-start.4
  242.7 2.6 copy-start.3
  250.1 0.7 copy-start.2
  250.1 1.2 copy-start.1
  253.3 15.0 %collective-permute-start = (bf16[512,512]{1,0:T(8,128)(2,1)S(1)}, bf16[512,512]{1,0:T(8,128)(2,1)S(1)}, u32[]{:S(2)}, u32[]{:S(2)}) collective-permute-start(bf16[512,512]{1,0:T(8,128)(2,1)S(1)} %gather_fusion), channel_id=1, source_target_pairs={{0,1},{1,0},{2,3},{3,2},{4,5},{5,4},{6,7},{7,6},{8,9},{9,8},{10,11... | collective-permute-start | bytes 1572872 | tf_op jit(solution)/shard_map/ppermute | solution.py:13
Sparse Core Ops, SparseCore 0:
  9.8 215.4 all-gather.1
  250.3 575.7 reduce-scatter.1
where the time goes:
time: 845 us
  waiting for transfers between devices  753 us (89%)
  blocking collectives  37.8 us (4%)
  matrix products  22 us (3%)
  between operations  14.7 us (2%)
    reduce_scatter x1, waiting for transfers between devices, local(): lax.psum_scatter(phrase_terms.reshape(total, width), 'batch', scatter_dim...  551 us
    all_gather x1, waiting for transfers between devices, local(): gathered = lax.all_gather(phrases, 'batch', axis=0, tiled=True)  189 us
    unnamed x1, blocking collectives  25.8 us
  transfers between devices with their start and end apart: 3, of which 3 were waited for; matrix products, arithmetic and copies ran while one was open for 1% of the time, Pallas kernels for 0%

commit v1 on v0

--- a/solution.py
+++ b/solution.py
@@ -34,7 +34,9 @@
         )
         return (match_part, phrase_part)
 
-    gathered = lax.all_gather(phrases, "batch", axis=0, tiled=True)
+    gathered = jnp.concatenate(
+        lax.all_to_all(jnp.stack([phrases] * lax.axis_size("batch")), "batch", 0, 0), axis=0
+    )
     total = gathered.shape[0]
     block_rows = math.gcd(total, 1024)
     num_blocks = total // block_rows

time: 845 us -> 694 us (0.82)
  waiting for transfers between devices: 753 us -> 563 us
  blocking collectives: 37.8 us -> 65.2 us
  starting transfers between devices: 3.16 us -> 15.6 us
    all_gather x1 -> x0, waiting for transfers between devices: 189 us -> none  [local(): gathered = lax.all_gather(phrases, 'batch', axis=0, tiled=True)]
    unnamed x1, blocking collectives: 25.8 us -> 52.9 us
    all_to_all x0 -> x1, starting transfers between devices: none -> 12.6 us  [local(): lax.all_to_all(jnp.stack([phrases] * lax.axis_size('batch')), 'batch', 0, 0)]
  transfers between devices with their start and end apart: 3 -> 3, of which waited for: 3 -> 2; matrix products, arithmetic and copies ran while one was open for 1% -> 1% of each run, Pallas kernels for 0% -> 0%
where the time goes in v1:
time: 694 us; the launch traced here: 693 us
  waiting for transfers between devices  563 us (81%)
  blocking collectives  65.2 us (9%)
  matrix products  19.3 us (3%)
  starting transfers between devices  15.6 us (2%)
  between operations  14.8 us (2%)
  local copies, waits for them, and re-layouts  8.5 us (1%)
    reduce_scatter x1, waiting for transfers between devices, local(): lax.psum_scatter(phrase_terms.reshape(total, width), 'batch', scatter_dim...  552 us
    unnamed x1, blocking collectives  52.9 us
  transfers between devices with their start and end apart: 3, of which 2 were waited for; matrix products, arithmetic and copies ran while one was open for 1% of the time, Pallas kernels for 0%

profile of v1, /device:TPU:0, one launch (start us, length us, event | category | flops | bytes accessed | tf_op | source)
XLA Modules:
  0.0 693.3 jit_solution(17507920172983041291)
XLA Ops:
  7.2 2.3 stack.2
  9.5 0.0 copy-start.3
  9.5 0.0 copy-start.2
  9.5 0.0 copy-start
  9.5 12.6 %all-to-all-start = ((bf16[128,16,512]{2,1,0:T(8,128)(2,1)}), bf16[128,16,512]{2,1,0:T(8,128)(2,1)S(1)}, u32[]{:S(2)}, u32[]{:S(2)}) async-start(bf16[128,16,512]{2,1,0:T(8,128)(2,1)} %stack.2), calls=%async_computation | async-start | bytes 4194304 | tf_op jit(solution)/shard_map/all_to_all | solution.py:38
  22.1 0.0 reduce-scatter.2.cloned.1.call-start
  22.2 0.0 copy-done.3
  22.2 0.6 dynamic-slice
  23.4 0.0 copy-done.2
  23.4 0.3 dynamic-update-slice
  23.7 52.9 %all-reduce = s32[2048]{0:T(1024)S(1)} all-reduce(s32[2048]{0:T(1024)S(1)} %dynamic-update-slice), channel_id=1, replica_groups=mesh['batch'=128,'crop'=2] {'batch'}, use_global_device_ids=true, to_apply=%add | all-reduce | flops 2048 | bytes 16384
  76.6 0.0 all-to-all-done
  76.7 0.0 copy-done
  76.7 22.0 %while.15 = (s32[]{:T(128)}, f32[1024,512]{1,0:T(8,128)}, f32[2,1024,512]{2,1,0:T(8,128)}, s32[2,1024]{1,0:T(2,128)S(1)}, bf16[2,1024,512]{2,1,0:T(8,128)(2,1)S(...) while((s32[]{:T(128)}, f32[1024,512]{1,0:T(8,128)}, ...), condition=%wide.region_1.2_spmd.clone, body=%wide.region_0.1_spmd.clone.sunk | while | flops 3234873344 | bytes 25186964 | solution.py:50
  76.7 2.5 fusion.38
  79.3 0.0 copy-start.4
  79.3 1.3 copy-done.4
  80.6 2.6 bitcast_dynamic-update-slice_fusion.2
  83.2 4.2 select_add_fusion.2
  87.4 2.5 fusion.38
  90.0 0.0 copy-start.4
  90.0 1.3 copy-done.4
  91.3 2.6 bitcast_dynamic-update-slice_fusion.2
  93.9 4.8 select_add_fusion.2
  98.7 0.0 reduce-scatter.2.cloned.1.call-update
  98.7 0.7 copy-done.1
  99.4 2.0 gather_fusion
  101.4 3.0 collective-permute-start
  104.3 11.2 %collective-permute-done = bf16[512,512]{1,0:T(8,128)(2,1)S(1)} collective-permute-done((bf16[512,512]{1,0:T(8,128)(2,1)S(1)}, bf16[512,512]{1,0:T(8,128)(2,1)S(1)}, u32[]{:S(2)}, u32[]{:S(2)}) %collective-permute-start) | collective-permute-done | bytes 524320 | tf_op jit(solution)/shard_map/ppermute | solution.py:13
  115.5 6.5 scatter_custom_fusion
  122.1 552.0 %reduce-scatter.2.cloned.1.call-done = f32[16,512]{1,0:T(8,128)} async-done(((f32[2048,512]{1,0:T(8,128)}), f32[16,512]{1,0:T(8,128)}) %reduce-scatter.2.cloned.1.call-update) | async-done | bytes 32784 | tf_op jit(solution)/shard_map/reduce_scatter | solution.py:53
  674.1 12.3 %psum.7 = f32[16,512]{1,0:T(8,128)} all-reduce(f32[16,512]{1,0:T(8,128)} %reduce-scatter.2.cloned.1.call-done), channel_id=1, replica_groups=mesh['batch'=128,'crop'=2] {'crop'}, use_global_device_ids=true, to_apply=%region_4.5 | all-reduce | flops 8192 | bytes 65536 | tf_op jit(solution)/shard_map/psum | solution.py:56
  (11 shorter events, 0.1 us)
Async XLA Ops:
  9.5 12.7 %copy-start.3 = (u32[256]{0:T(256)S(1)}, u32[256]{0:T(256)}, u32[]{:S(2)}) copy-start(u32[256]{0:T(256)} %constant.75) | copy-start | bytes 3076
  9.5 14.0 %copy-start.2 = (s32[16]{0:T(128)S(1)}, s32[16]{0:T(128)}, u32[]{:S(2)}) copy-start(s32[16]{0:T(128)} %param.8) | copy-start | bytes 196
  9.5 67.2 %copy-start = (bf16[1,1024,512]{2,1,0:T(8,128)(2,1)S(1)}, bf16[1,1024,512]{2,1,0:T(8,128)(2,1)}, u32[]{:S(2)}) copy-start(bf16[1,1024,512]{2,1,0:T(8,128)(2,1)} %param.6) | copy-start | bytes 3145732
  9.5 67.2 %all-to-all-start = ((bf16[128,16,512]{2,1,0:T(8,128)(2,1)}), bf16[128,16,512]{2,1,0:T(8,128)(2,1)S(1)}, u32[]{:S(2)}, u32[]{:S(2)}) async-start(bf16[128,16,512]{2,1,0:T(8,128)(2,1)} %stack.2), calls=%async_computation | async-start | bytes 4194304 | tf_op jit(solution)/shard_map/all_to_all | solution.py:38
  22.1 652.0 %reduce-scatter.2.cloned.1.call-start = ((), (), s32[]{:S(2)}) async-start(), calls=%async_computation.2 | async-start | bytes 4227072 | tf_op jit(solution)/shard_map/reduce_scatter | solution.py:53
  79.3 1.3 copy-start.4
  90.0 1.3 copy-start.4
  98.7 0.7 copy-start.1
  101.4 14.2 %collective-permute-start = (bf16[512,512]{1,0:T(8,128)(2,1)S(1)}, bf16[512,512]{1,0:T(8,128)(2,1)S(1)}, u32[]{:S(2)}, u32[]{:S(2)}) collective-permute-start(bf16[512,512]{1,0:T(8,128)(2,1)S(1)} %gather_fusion), channel_id=1, source_target_pairs={{0,1},{1,0},{2,3},{3,2},{4,5},{5,4},{6,7},{7,6},{8,9},{9,8},{10,11... | collective-permute-start | bytes 1572872 | tf_op jit(solution)/shard_map/ppermute | solution.py:13
Sparse Core Ops, SparseCore 0:
  98.8 575.2 reduce-scatter.1
